TPU v7x, 256 devices: a whole 4x4x8 slice. The times are simulated.
256 devices in a mesh: sample: 16 (over z, core), expert: 16 (over y, x).
Axes of the slice: x: 4, y: 4, z: 8, core: 2. Of those that a mesh axis runs over, the one named last changes fastest.
Arguments:
- queries: bfloat16 [128, 16, 8192], P('expert', 'sample'), may hold values from -8 to 8
- prompt_kv: bfloat16 [128, 1024, 1024], P('expert', 'sample'), may hold values from -8 to 8
- gen_kv: bfloat16 [128, 16, 32, 1024], P('expert', 'sample'), may hold values from -4 to 4
- gen_lengths: int32 [128, 16], P('expert', 'sample'), may hold values from 1 to 32, 256 in all within a row
- out_proj: bfloat16 [8192, 4096], P(None, 'sample'), may hold values from -1 to 1
- residual: bfloat16 [128, 16, 4096], P('expert', None, 'sample'), may hold values from -160 to 160
- norm_gain: float32 [4096], P('sample'), may hold values from 0.1 to 1.9
- w_gate_up: bfloat16 [48, 4096, 3072], P('expert', 'sample'), may hold values from -0.09375 to 0.09375
- w_down: bfloat16 [48, 1536, 4096], P('expert', None, 'sample'), may hold values from -0.15625 to 0.15625
- routes: int32 [128, 16, 8], P('expert'), may hold values from 0 to 47, all different within a row; in each aligned block of 128 rows (0 to 127, 128 to 255, ..., all dimensions but the last counted through in order) at most 26 rows name the same one
- route_probs: float32 [128, 16, 8], P('expert'), may hold values from 0.1 to 1
Outputs:
- mixed: bfloat16 [128, 16, 4096], P('expert', None, 'sample')
- expert_out: bfloat16 [128, 16, 4096], P('expert', None, 'sample')
Inputs may be any that keep to these rules, and one draw needn't show every extreme that they name: `gen_lengths`: in each prompt, at least one sample has 32 generated tokens. `routes`: each row names 8 different experts. Among the 128 rows of the prompts of one index of expert, no expert is named by more than 26 rows, a bound that some block reaches.
All inputs are finite; a program needn't handle non-finite values. No bound on the sum of `gen_lengths` on one device may be relied on, other than what follows from the above.
Results may differ from a plain program's by a relative error of at most 0.028.
Values may be sent and summed in bfloat16 or wider, within the bound.
A program may use at most 128 MiB of HBM per device.

v0:
```python
import jax
import jax.numpy as jnp
from jax import lax
from jax.sharding import PartitionSpec as P

D = 4096
FF = 1536
QHEADS = 64
KVHEADS = 4
HDIM = 128
TOPK = 8
EXP_COL = 3
NEGATIVE = -1e30
EPSILON = 1e-06


def absorb(carried, scores, value_rows):
    highest = jnp.maximum(carried[0], jnp.max(scores, axis=-1))
    rescale = jnp.exp(carried[0] - highest)
    weights = jnp.exp(scores - highest[..., None])
    weight_sum = carried[1] * rescale + jnp.sum(weights, axis=-1)
    numerator = carried[2] * rescale[..., None] + jnp.einsum(
        "brhgn,bnhd->brhgd",
        weights,
        value_rows.astype(jnp.float32),
        precision=lax.Precision.HIGHEST,
    )
    return (highest, weight_sum, numerator)


def split_cache(cache):
    kv_width = KVHEADS * HDIM
    prompts_here = cache.shape[0]
    length = cache.shape[1]
    key_rows = cache[:, :, :kv_width].reshape(prompts_here, length, KVHEADS, HDIM)
    value_rows = cache[:, :, kv_width:].reshape(prompts_here, length, KVHEADS, HDIM)
    return (key_rows, value_rows)


def score_rows(query, key_rows):
    return jnp.einsum(
        "brhgd,bnhd->brhgn", query, key_rows, preferred_element_type=jnp.float32
    ) * HDIM ** (-0.5)


def empty_state(shape):
    return (
        jnp.full(shape, NEGATIVE, jnp.float32),
        jnp.zeros(shape, jnp.float32),
        jnp.zeros(shape + (HDIM,), jnp.float32),
    )


def on_device(
    queries,
    prompt_kv,
    gen_kv,
    gen_lengths,
    out_proj,
    residual,
    norm_gain,
    w_gate_up,
    w_down,
    routes,
    route_probs,
):
    prompts_here = queries.shape[0]
    groups = QHEADS // KVHEADS
    samples = lax.axis_size("sample")
    width = residual.shape[2]
    own_query = queries.reshape(prompts_here, 1, KVHEADS, groups, HDIM)
    gen_keys, gen_values = split_cache(gen_kv[:, 0])
    positions = jnp.arange(gen_kv.shape[2], dtype=jnp.int32)
    valid = (positions[None, :] < gen_lengths)[:, None, None, None, :]
    gen_scores = jnp.where(valid, score_rows(own_query, gen_keys), NEGATIVE)
    own_state = absorb(empty_state((prompts_here, 1, KVHEADS, groups)), gen_scores, gen_values)
    key_rows, value_rows = split_cache(lax.all_gather(prompt_kv, "sample", axis=1, tiled=True))
    merged = absorb(own_state, score_rows(own_query, key_rows), value_rows)
    attended = (
        (merged[2] / merged[1][..., None])
        .astype(jnp.bfloat16)
        .reshape(prompts_here, 1, QHEADS * HDIM)
    )
    projected = jnp.einsum(
        "bnq,qd->bnd",
        lax.all_gather(attended, "sample", axis=1, tiled=True),
        out_proj,
        preferred_element_type=jnp.float32,
    )
    mixed = projected.astype(jnp.bfloat16)
    stream = residual.astype(jnp.float32) + projected
    squares = lax.psum(jnp.sum(stream * stream, axis=-1), "sample")
    factor = lax.rsqrt(squares / D + EPSILON)
    row_count = prompts_here * samples
    normed = (stream * factor[..., None] * norm_gain).astype(jnp.bfloat16).reshape(row_count, width)
    owners = lax.axis_size("expert")
    experts_all = EXP_COL * owners
    capacity = 5 * prompts_here * samples * TOPK // (4 * experts_all)
    expert_ids = routes.reshape(row_count, TOPK)
    route_weight = route_probs.reshape(row_count, TOPK)
    expert_hits = jnp.sum(
        (expert_ids[:, :, None] == jnp.arange(experts_all, dtype=jnp.int32)[None, None, :]).astype(
            jnp.int32
        ),
        axis=1,
    )
    before = jnp.cumsum(expert_hits, axis=0) - expert_hits
    arrival = jnp.take_along_axis(before, expert_ids, axis=1)
    slot_index = (expert_ids * capacity + arrival).reshape(-1)
    outgoing = (
        jnp.zeros((experts_all * capacity, width), jnp.bfloat16)
        .at[slot_index]
        .set(jnp.repeat(normed, TOPK, axis=0))
    )
    outgoing = outgoing.reshape(owners, EXP_COL, capacity, width)
    partial_sums = jnp.einsum(
        "sjcd,jdf->sjcf",
        lax.all_to_all(outgoing, "expert", split_axis=0, concat_axis=0, tiled=True),
        w_gate_up,
        preferred_element_type=jnp.float32,
    )
    gate_up = lax.psum(partial_sums.astype(jnp.bfloat16), "sample").astype(jnp.float32)
    activated = (jax.nn.silu(gate_up[..., :FF]) * gate_up[..., FF:]).astype(jnp.bfloat16)
    finished = jnp.einsum(
        "sjcf,jfd->sjcd", activated, w_down, preferred_element_type=jnp.float32
    ).astype(jnp.bfloat16)
    returned = lax.all_to_all(finished, "expert", split_axis=0, concat_axis=0, tiled=True)
    picked = jnp.take(returned.reshape(experts_all * capacity, width), slot_index, axis=0).reshape(
        row_count, TOPK, width
    )
    combined = jnp.sum(picked.astype(jnp.float32) * route_weight[:, :, None], axis=1)
    expert_out = combined.astype(jnp.bfloat16).reshape(prompts_here, samples, width)
    return (mixed, expert_out)


def solution(mesh):
    placed = (
        P("expert", "sample", None),
        P("expert", "sample", None),
        P("expert", "sample", None, None),
        P("expert", "sample"),
        P(None, "sample"),
        P("expert", None, "sample"),
        P("sample"),
        P("expert", "sample", None),
        P("expert", None, "sample"),
        P("expert", None, None),
        P("expert", None, None),
    )
    return jax.shard_map(
        on_device,
        mesh=mesh,
        in_specs=placed,
        out_specs=(P("expert", None, "sample"), P("expert", None, "sample")),
        check_vma=False,
    )
```

profile of v0, /device:TPU:97, one launch (start us, length us, event | category | flops | bytes accessed | tf_op | source)
XLA Modules:
  0.0 452.4 jit_solution(12887853357959558005)
XLA Ops:
  7.2 2.9 copy.82
  10.2 0.7 iota_compare_fusion.1
  11.0 1.1 slice_bitcast_fusion
  12.0 1.2 fusion.59
  13.3 94.0 %all-gather.3.cloned.1.call-done = bf16[8,1024,1024]{2,0,1:T(8,128)(2,1)} async-done(((bf16[8,64,1024]{2,0,1:T(8,128)(2,1)}), bf16[8,1024,1024]{2,0,1:T(8,128)(2,1)}) %all-gather.3.cloned.1.call-update) | async-done | bytes 16777232 | tf_op jit(solution)/shard_map/all_gather | solution.py:77
  107.3 11.3 %fusion.58 = (bf16[8,1024,512]{2,0,1:T(8,128)(2,1)}, bf16[8,1024,512]{2,0,1:T(8,128)(2,1)}) fusion(bf16[8,1024,1024]{2,0,1:T(8,128)(2,1)} %all-gather.3.cloned.1.call-done), kind=kLoop, calls=%fused_computation.79 | loop fusion | bytes 33554432 | tf_op jit(solution)/shard_map/slice | solution.py:35
  118.6 12.3 %copy.109 = bf16[8,1024,512]{1,2,0:T(8,128)(2,1)} copy(bf16[8,1024,512]{2,0,1:T(8,128)(2,1)} %get-tuple-element.8) | data formatting | bytes 16777216
  130.9 6.0 %bitcast_reduce_fusion = (f32[8,4,16]{2,1,0:T(4,128)S(1)}, f32[8,4,1024,16]{2,3,1,0:T(8,128)}) fusion(bf16[8,1024,4,128]{1,3,2,0:T(8,128)(2,1)} %bitcast.118, bf16[8,4,16,128]{3,0,2,1:T(8,128)(2,1)S(1)} %bitcast.124), kind=kOutput, calls=%fused_computation.14 | convolution fusion | flops 135265792 | bytes 10618880 | tf_op jit(solution)/shard_map/brhgd,bnhd->brhgn/dot_general | solution.py:41
  136.8 12.2 %copy.110 = bf16[8,1024,512]{1,2,0:T(8,128)(2,1)} copy(bf16[8,1024,512]{2,0,1:T(8,128)(2,1)} %get-tuple-element.9) | data formatting | bytes 16777216
  149.1 2.2 fusion.10
  151.4 9.0 %fusion.22 = f32[8,4,128,1,16]{2,4,1,0,3:T(8,128)S(1)} fusion(bf16[8,1024,4,128]{1,3,2,0:T(8,128)(2,1)} %bitcast.117, f32[8,4,1024,16]{2,3,1,0:T(8,128)S(1)} %copy-done.1, f32[8,4,16]{2,1,0:T(4,128)S(1)} %get-tuple-element.15), kind=kOutput, calls=%fused_computation.19 | convolution fusion | flops 806354944 | bytes 10749952 | tf_op jit(solution)/shard_map/brhgn,bnhd->brhgd/dot_general | solution.py:22
  160.7 0.4 fusion.33
  161.2 0.7 reshape.292
  162.9 7.1 %gather_fusion.1 = s32[1024]{0:T(1024)S(1)} fusion(s32[128,48]{1,0:T(8,128)S(1)} %sub.53, s32[1024]{0:T(1024)S(1)} %reshape.308), kind=kCustom, calls=%fused_computation.1 | custom fusion | bytes 16384 | tf_op jit(solution)/shard_map/jit(take_along_axis)/gather | solution.py:108
  170.0 30.0 %all-gather.5.cloned.1.call-done = bf16[8,16,8192]{2,0,1:T(8,128)(2,1)} async-done(((bf16[8,1,8192]{2,0,1:T(8,128)(2,1)}), bf16[8,16,8192]{2,0,1:T(8,128)(2,1)}) %all-gather.5.cloned.1.call-update) | async-done | bytes 2097168 | tf_op jit(solution)/shard_map/all_gather | solution.py:86
  200.0 3.6 multiply_reduce_fusion.1
  203.6 23.5 %psum.14 = f32[8,16]{0,1:T(8,128)S(1)} all-reduce(f32[8,16]{0,1:T(8,128)S(1)} %get-tuple-element.21), channel_id=1, replica_groups=mesh['sample'=16,'expert'=16] {'sample'}, use_global_device_ids=true, to_apply=%region_7.8 | all-reduce | flops 128 | bytes 1024 | tf_op jit(solution)/shard_map/psum | solution.py:92
  227.3 5.8 %scatter_custom_fusion = bf16[1248,256]{1,0:T(8,128)(2,1)} fusion(s32[1024]{0:T(1024)S(1)} %bitcast.126, bf16[]{:T(256)} %constant.35.clone.1, bf16[128,256]{1,0:T(8,128)(2,1)S(1)} %bitcast.121), kind=kCustom, calls=%fused_computation.36 | custom fusion | bytes 704514 | tf_op jit(solution)/shard_map/scatter | solution.py:113
  233.1 1.3 reshape.298
  234.3 21.4 %all_to_all.10 = bf16[16,3,26,256]{3,2,1,0:T(8,128)(2,1)S(1)} all-to-all(bf16[16,3,26,256]{3,2,1,0:T(8,128)(2,1)S(1)} %reshape.298), channel_id=1, replica_groups=mesh['sample'=16,'expert'=16] {'expert'}, dimensions={0} | all-to-all | bytes 1277952 | tf_op jit(solution)/shard_map/all_to_all | solution.py:118
  255.7 7.5 %convert_bitcast_fusion = bf16[16,3,26,3072]{3,2,0,1:T(8,128)(2,1)} fusion(bf16[3,256,3072]{2,1,0:T(8,128)(2,1)} %param.18, bf16[16,3,26,256]{3,2,1,0:T(8,128)(2,1)S(1)} %all_to_all.10), kind=kOutput, calls=%fused_computation.5 | convolution fusion | flops 1966768128 | bytes 13025280 | tf_op jit(solution)/shard_map/sjcd,jdf->sjcf/dot_general | solution.py:116
  263.2 133.9 %all-reduce.2.cloned.1.call-done = bf16[16,3,26,3072]{3,2,0,1:T(8,128)(2,1)} async-done(((bf16[16,3,26,3072]{3,2,0,1:T(8,128)(2,1)}), bf16[16,3,26,3072]{3,2,0,1:T(8,128)(2,1)}) %all-reduce.2.cloned.1.call-update) | async-done | bytes 7667728 | tf_op jit(solution)/shard_map/psum | solution.py:122
  397.1 12.4 %convert_element_type.49 = f32[16,3,26,3072]{3,2,0,1:T(8,128)} convert(bf16[16,3,26,3072]{3,2,0,1:T(8,128)(2,1)} %all-reduce.2.cloned.1.call-done) | non-fusion elementwise | flops 3833856 | bytes 23003136 | tf_op jit(solution)/shard_map/convert_element_type | solution.py:122
  409.6 8.0 %fusion.17 = bf16[16,3,26,256]{3,2,0,1:T(8,128)(2,1)S(1)} fusion(bf16[3,1536,256]{2,1,0:T(8,128)(2,1)S(1)} %copy-done, f32[16,3,26,3072]{3,2,0,1:T(8,128)} %convert_element_type.49), kind=kOutput, calls=%fused_computation.18 | convolution fusion | flops 993288192 | bytes 18333696 | tf_op jit(solution)/shard_map/sjcf,jfd->sjcd/dot_general | solution.py:124
  417.6 1.0 copy.99
  418.5 6.6 %all-to-all-start.1 = ((bf16[16,3,26,256]{3,2,1,0:T(8,128)(2,1)}), bf16[16,3,26,256]{3,2,1,0:T(8,128)(2,1)}, u32[]{:S(2)}, u32[]{:S(2)}) async-start(bf16[16,3,26,256]{3,2,1,0:T(8,128)(2,1)} %copy.99), calls=%async_computation.1 | async-start | bytes 1572864 | tf_op jit(solution)/shard_map/all_to_all | solution.py:127
  425.4 0.7 copy.107
  426.1 0.6 copy.102
  426.7 11.9 %all-to-all-done.1 = bf16[16,3,26,256]{3,2,1,0:T(8,128)(2,1)} async-done(((bf16[16,3,26,256]{3,2,1,0:T(8,128)(2,1)}), bf16[16,3,26,256]{3,2,1,0:T(8,128)(2,1)}, u32[]{:S(2)}, u32[]{:S(2)}) %all-to-all-start.1) | async-done | bytes 639008 | tf_op jit(solution)/shard_map/all_to_all | solution.py:127
  438.7 1.3 reshape.299
  440.0 3.9 gather_fusion
  443.9 1.9 multiply_reduce_fusion
  (44 shorter events, 1.8 us)
Async XLA Ops:
  7.2 402.4 %copy-start = (bf16[3,1536,256]{2,1,0:T(8,128)(2,1)S(1)}, bf16[3,1536,256]{2,1,0:T(8,128)(2,1)}, u32[]{:S(2)}) copy-start(bf16[3,1536,256]{2,1,0:T(8,128)(2,1)} %param.19) | copy-start | bytes 7077892
  7.2 100.1 %all-gather.3.cloned.1.call-start = ((), (), s32[]{:S(2)}) async-start(), calls=%async_computation.2 | async-start | bytes 17825792 | tf_op jit(solution)/shard_map/all_gather | solution.py:77
  10.2 189.8 %all-gather.5.cloned.1.call-start = ((), (), s32[]{:S(2)}) async-start(), calls=%async_computation.3 | async-start | bytes 2228224 | tf_op jit(solution)/shard_map/all_gather | solution.py:86
  118.6 12.3 %copy-start.3 = (bf16[8,1,8192]{2,0,1:T(8,128)(2,1)S(1)}, bf16[8,1,8192]{2,0,1:T(8,128)(2,1)}, u32[]{:S(2)}) copy-start(bf16[8,1,8192]{2,0,1:T(8,128)(2,1)} %param.11) | copy-start | bytes 393220
  149.1 2.3 copy-start.1
  151.4 10.6 %copy-start.4 = (s32[8,16,8]{1,2,0:T(8,128)S(1)}, s32[8,16,8]{1,2,0:T(8,128)}, u32[]{:S(2)}) copy-start(s32[8,16,8]{1,2,0:T(8,128)} %param.20) | copy-start | bytes 12292
  161.9 235.2 %all-reduce.2.cloned.1.call-start = ((), (), s32[]{:S(2)}) async-start(), calls=%async_computation.4 | async-start | bytes 18874368 | tf_op jit(solution)/shard_map/psum | solution.py:122
  162.8 37.2 %copy-start.2 = (bf16[8,16,256]{2,1,0:T(8,128)(2,1)S(1)}, bf16[8,16,256]{2,1,0:T(8,128)(2,1)}, u32[]{:S(2)}) copy-start(bf16[8,16,256]{2,1,0:T(8,128)(2,1)} %param.16) | copy-start | bytes 196612
  169.9 57.2 %copy-start.6 = (f32[256]{0:T(256)S(1)}, f32[256]{0:T(256)}, u32[]{:S(2)}) copy-start(f32[256]{0:T(256)} %param.17) | copy-start | bytes 3076
  409.6 15.8 %copy-start.5 = (f32[8,16,8]{1,2,0:T(8,128)S(1)}, f32[8,16,8]{1,2,0:T(8,128)}, u32[]{:S(2)}) copy-start(f32[8,16,8]{1,2,0:T(8,128)} %param.21) | copy-start | bytes 12292
  418.5 20.2 %all-to-all-start.1 = ((bf16[16,3,26,256]{3,2,1,0:T(8,128)(2,1)}), bf16[16,3,26,256]{3,2,1,0:T(8,128)(2,1)}, u32[]{:S(2)}, u32[]{:S(2)}) async-start(bf16[16,3,26,256]{3,2,1,0:T(8,128)(2,1)} %copy.99), calls=%async_computation.1 | async-start | bytes 1572864 | tf_op jit(solution)/shard_map/all_to_all | solution.py:127
Sparse Core Ops, SparseCore 0:
  10.3 96.8 all-gather.2
  162.0 37.9 all-gather.4
  263.3 133.7 all-reduce.1
where the time goes:
time: 453 us; the launch traced here: 452 us
  waiting for transfers between devices  270 us (60%)
  local copies, waits for them, and re-layouts  63.1 us (14%)
  blocking collectives  44.9 us (10%)
  matrix products  35.7 us (8%)
  other arithmetic  18.1 us (4%)
  between operations  14 us (3%)
  starting transfers between devices  6.69 us (1%)
    psum x1, waiting for transfers between devices, on_device(): lax.psum(partial_sums.astype(jnp.bfloat16), 'sample').astype(jnp.float32)  134 us
    all_gather x1, waiting for transfers between devices, on_device(): lax.all_gather(prompt_kv, 'sample', axis=1, tiled=True)  94 us
    all_gather x1, waiting for transfers between devices, on_device(): lax.all_gather(attended, 'sample', axis=1, tiled=True)  30 us
    unnamed x21, local copies, waits for them, and re-layouts  29.3 us
    psum x1, blocking collectives, on_device(): squares = lax.psum(jnp.sum(stream * stream, axis=-1), 'sample')  23.5 us
    all_to_all x1, blocking collectives, on_device(): lax.all_to_all(outgoing, 'expert', split_axis=0, concat_axis=0, tiled=True)  21.4 us
    convert_element_type x1, other arithmetic, on_device(): lax.psum(partial_sums.astype(jnp.bfloat16), 'sample').astype(jnp.float32)  12.4 us
    all_to_all x1, waiting for transfers between devices, on_device(): lax.all_to_all(finished, 'expert', split_axis=0, concat_axis=0, tiled=True)  11.9 us
  transfers between devices with their start and end apart: 4, of which 4 were waited for; matrix products, arithmetic and copies ran while one was open for 3% of the time, Pallas kernels for 0%

commit v1 on v0

--- a/solution.py
+++ b/solution.py
@@ -12,6 +12,13 @@
 EXP_COL = 3
 NEGATIVE = -1e30
 EPSILON = 1e-06
+
+
+def gather_over(shard, name, dim):
+    size = lax.axis_size(name)
+    blocks = jnp.stack([shard for _ in range(size)])
+    blocks = lax.all_to_all(blocks, name, split_axis=0, concat_axis=0)
+    return jnp.concatenate(blocks, axis=dim)
 
 
 def absorb(carried, scores, value_rows):
@@ -83,7 +90,7 @@
     )
     projected = jnp.einsum(
         "bnq,qd->bnd",
-        lax.all_gather(attended, "sample", axis=1, tiled=True),
+        gather_over(attended, "sample", 1),
         out_proj,
         preferred_element_type=jnp.float32,
     )

time: 453 us -> 471 us (1.040)
  waiting for transfers between devices: 270 us -> 281 us
  starting transfers between devices: 6.69 us -> 11.8 us
    all_to_all x0 -> x1, waiting for transfers between devices: none -> 40.7 us  [gather_over(): blocks = lax.all_to_all(blocks, name, split_axis=0, concat_axis=0)]
    all_gather x1 -> x0, waiting for transfers between devices: 30 us -> none  [on_device(): lax.all_gather(attended, 'sample', axis=1, tiled=True)]
    all_to_all x0 -> x1, starting transfers between devices: none -> 5.16 us  [gather_over(): blocks = lax.all_to_all(blocks, name, split_axis=0, concat_axis=0)]
where the time goes in v1:
time: 471 us; the launch traced here: 470 us
  waiting for transfers between devices  281 us (60%)
  local copies, waits for them, and re-layouts  63.9 us (14%)
  blocking collectives  44.9 us (10%)
  matrix products  35.7 us (8%)
  other arithmetic  18.1 us (4%)
  between operations  14.3 us (3%)
  starting transfers between devices  11.8 us (3%)
    psum x1, waiting for transfers between devices, on_device(): lax.psum(partial_sums.astype(jnp.bfloat16), 'sample').astype(jnp.float32)  134 us
    all_gather x1, waiting for transfers between devices, on_device(): lax.all_gather(prompt_kv, 'sample', axis=1, tiled=True)  94 us
    all_to_all x1, waiting for transfers between devices, gather_over(): blocks = lax.all_to_all(blocks, name, split_axis=0, concat_axis=0)  40.7 us
    unnamed x21, local copies, waits for them, and re-layouts  29.3 us
    psum x1, blocking collectives, on_device(): squares = lax.psum(jnp.sum(stream * stream, axis=-1), 'sample')  23.5 us
    all_to_all x1, blocking collectives, on_device(): lax.all_to_all(outgoing, 'expert', split_axis=0, concat_axis=0, tiled=True)  21.4 us
    convert_element_type x1, other arithmetic, on_device(): lax.psum(partial_sums.astype(jnp.bfloat16), 'sample').astype(jnp.float32)  12.4 us
    all_to_all x1, waiting for transfers between devices, on_device(): lax.all_to_all(finished, 'expert', split_axis=0, concat_axis=0, tiled=True)  11.9 us
  transfers between devices with their start and end apart: 4, of which 4 were waited for; matrix products, arithmetic and copies ran while one was open for 3% of the time, Pallas kernels for 0%

profile of v1, /device:TPU:97, one launch (start us, length us, event | category | flops | bytes accessed | tf_op | source)
XLA Modules:
  0.0 469.6 jit_solution(1622135046852311869)
XLA Ops:
  7.2 2.9 copy.81
  10.2 0.7 iota_compare_fusion.1
  10.9 1.1 slice_bitcast_fusion
  12.0 1.2 fusion.60
  13.2 94.0 %all-gather.2.cloned.1.call-done = bf16[8,1024,1024]{2,0,1:T(8,128)(2,1)} async-done(((bf16[8,64,1024]{2,0,1:T(8,128)(2,1)}), bf16[8,1024,1024]{2,0,1:T(8,128)(2,1)}) %all-gather.2.cloned.1.call-update) | async-done | bytes 16777232 | tf_op jit(solution)/shard_map/all_gather | solution.py:84
  107.3 11.3 %fusion.59 = (bf16[8,1024,512]{2,0,1:T(8,128)(2,1)}, bf16[8,1024,512]{2,0,1:T(8,128)(2,1)}) fusion(bf16[8,1024,1024]{2,0,1:T(8,128)(2,1)} %all-gather.2.cloned.1.call-done), kind=kLoop, calls=%fused_computation.80 | loop fusion | bytes 33554432 | tf_op jit(solution)/shard_map/slice | solution.py:42
  118.6 12.3 %copy.109 = bf16[8,1024,512]{1,2,0:T(8,128)(2,1)} copy(bf16[8,1024,512]{2,0,1:T(8,128)(2,1)} %get-tuple-element.8) | data formatting | bytes 16777216
  130.9 6.0 %bitcast_reduce_fusion = (f32[8,4,16]{2,1,0:T(4,128)S(1)}, f32[8,4,1024,16]{2,3,1,0:T(8,128)}) fusion(bf16[8,1024,4,128]{1,3,2,0:T(8,128)(2,1)} %bitcast.126, bf16[8,4,16,128]{3,0,2,1:T(8,128)(2,1)S(1)} %bitcast.132), kind=kOutput, calls=%fused_computation.15 | convolution fusion | flops 135265792 | bytes 10618880 | tf_op jit(solution)/shard_map/brhgd,bnhd->brhgn/dot_general | solution.py:48
  136.8 12.2 %copy.110 = bf16[8,1024,512]{1,2,0:T(8,128)(2,1)} copy(bf16[8,1024,512]{2,0,1:T(8,128)(2,1)} %get-tuple-element.9) | data formatting | bytes 16777216
  149.1 2.2 fusion.11
  151.4 9.0 %fusion.23 = f32[8,4,128,1,16]{2,4,1,0,3:T(8,128)S(1)} fusion(bf16[8,1024,4,128]{1,3,2,0:T(8,128)(2,1)} %bitcast.125, f32[8,4,1024,16]{2,3,1,0:T(8,128)S(1)} %copy-done.1, f32[8,4,16]{2,1,0:T(4,128)S(1)} %get-tuple-element.15), kind=kOutput, calls=%fused_computation.20 | convolution fusion | flops 806354944 | bytes 10749952 | tf_op jit(solution)/shard_map/brhgn,bnhd->brhgd/dot_general | solution.py:29
  161.2 1.5 stack.3
  162.7 5.2 %all-to-all-start = ((bf16[16,8,1,8192]{3,1,2,0:T(8,128)(2,1)}), bf16[16,8,1,8192]{3,1,2,0:T(8,128)(2,1)}, u32[]{:S(2)}, u32[]{:S(2)}) async-start(bf16[16,8,1,8192]{3,1,2,0:T(8,128)(2,1)} %stack.3), calls=%async_computation | async-start | bytes 4194304 | tf_op jit(solution)/shard_map/all_to_all | solution.py:20
  168.8 7.1 %gather_fusion.1 = s32[1024]{0:T(1024)S(1)} fusion(s32[128,48]{1,0:T(8,128)S(1)} %sub.53, s32[1024]{0:T(1024)S(1)} %reshape.316), kind=kCustom, calls=%fused_computation.1 | custom fusion | bytes 16384 | tf_op jit(solution)/shard_map/jit(take_along_axis)/gather | solution.py:115
  175.9 40.7 %all-to-all-done = bf16[16,8,1,8192]{3,1,2,0:T(8,128)(2,1)} async-done(((bf16[16,8,1,8192]{3,1,2,0:T(8,128)(2,1)}), bf16[16,8,1,8192]{3,1,2,0:T(8,128)(2,1)}, u32[]{:S(2)}, u32[]{:S(2)}) %all-to-all-start) | async-done | bytes 2097184 | tf_op jit(solution)/shard_map/all_to_all | solution.py:20
  216.7 3.6 multiply_reduce_fusion.1
  220.3 23.5 %psum.14 = f32[8,16]{0,1:T(8,128)S(1)} all-reduce(f32[8,16]{0,1:T(8,128)S(1)} %get-tuple-element.21), channel_id=1, replica_groups=mesh['sample'=16,'expert'=16] {'sample'}, use_global_device_ids=true, to_apply=%region_7.8 | all-reduce | flops 128 | bytes 1024 | tf_op jit(solution)/shard_map/psum | solution.py:99
  243.9 5.8 %scatter_custom_fusion = bf16[1248,256]{1,0:T(8,128)(2,1)} fusion(s32[1024]{0:T(1024)S(1)} %bitcast.134, bf16[]{:T(256)} %constant.35.clone.1, bf16[128,256]{1,0:T(8,128)(2,1)S(1)} %bitcast.129), kind=kCustom, calls=%fused_computation.37 | custom fusion | bytes 704514 | tf_op jit(solution)/shard_map/scatter | solution.py:120
  249.7 1.3 reshape.306
  251.0 21.4 %all_to_all.15 = bf16[16,3,26,256]{3,2,1,0:T(8,128)(2,1)S(1)} all-to-all(bf16[16,3,26,256]{3,2,1,0:T(8,128)(2,1)S(1)} %reshape.306), channel_id=1, replica_groups=mesh['sample'=16,'expert'=16] {'expert'}, dimensions={0} | all-to-all | bytes 1277952 | tf_op jit(solution)/shard_map/all_to_all | solution.py:125
  272.4 7.5 %convert_bitcast_fusion = bf16[16,3,26,3072]{3,2,0,1:T(8,128)(2,1)} fusion(bf16[3,256,3072]{2,1,0:T(8,128)(2,1)} %param.18, bf16[16,3,26,256]{3,2,1,0:T(8,128)(2,1)S(1)} %all_to_all.15), kind=kOutput, calls=%fused_computation.5 | convolution fusion | flops 1966768128 | bytes 13025280 | tf_op jit(solution)/shard_map/sjcd,jdf->sjcf/dot_general | solution.py:123
  279.9 134.1 %all-reduce.2.cloned.1.call-done = bf16[16,3,26,3072]{3,2,0,1:T(8,128)(2,1)} async-done(((bf16[16,3,26,3072]{3,2,0,1:T(8,128)(2,1)}), bf16[16,3,26,3072]{3,2,0,1:T(8,128)(2,1)}) %all-reduce.2.cloned.1.call-update) | async-done | bytes 7667728 | tf_op jit(solution)/shard_map/psum | solution.py:129
  414.0 12.4 %convert_element_type.49 = f32[16,3,26,3072]{3,2,0,1:T(8,128)} convert(bf16[16,3,26,3072]{3,2,0,1:T(8,128)(2,1)} %all-reduce.2.cloned.1.call-done) | non-fusion elementwise | flops 3833856 | bytes 23003136 | tf_op jit(solution)/shard_map/convert_element_type | solution.py:129
  426.4 8.0 %fusion.18 = bf16[16,3,26,256]{3,2,0,1:T(8,128)(2,1)S(1)} fusion(bf16[3,1536,256]{2,1,0:T(8,128)(2,1)S(1)} %copy-done, f32[16,3,26,3072]{3,2,0,1:T(8,128)} %convert_element_type.49), kind=kOutput, calls=%fused_computation.19 | convolution fusion | flops 993288192 | bytes 18333696 | tf_op jit(solution)/shard_map/sjcf,jfd->sjcd/dot_general | solution.py:131
  434.4 1.0 copy.99
  435.4 6.6 %all-to-all-start.2 = ((bf16[16,3,26,256]{3,2,1,0:T(8,128)(2,1)}), bf16[16,3,26,256]{3,2,1,0:T(8,128)(2,1)}, u32[]{:S(2)}, u32[]{:S(2)}) async-start(bf16[16,3,26,256]{3,2,1,0:T(8,128)(2,1)} %copy.99), calls=%async_computation.2 | async-start | bytes 1572864 | tf_op jit(solution)/shard_map/all_to_all | solution.py:134
  442.2 0.7 copy.107
  443.0 0.6 copy.102
  443.6 11.9 %all-to-all-done.2 = bf16[16,3,26,256]{3,2,1,0:T(8,128)(2,1)} async-done(((bf16[16,3,26,256]{3,2,1,0:T(8,128)(2,1)}), bf16[16,3,26,256]{3,2,1,0:T(8,128)(2,1)}, u32[]{:S(2)}, u32[]{:S(2)}) %all-to-all-start.2) | async-done | bytes 639008 | tf_op jit(solution)/shard_map/all_to_all | solution.py:134
  455.5 1.3 reshape.307
  456.8 3.9 gather_fusion
  460.8 1.9 multiply_reduce_fusion
  (44 shorter events, 2.2 us)
Async XLA Ops:
  7.2 419.2 %copy-start = (bf16[3,1536,256]{2,1,0:T(8,128)(2,1)S(1)}, bf16[3,1536,256]{2,1,0:T(8,128)(2,1)}, u32[]{:S(2)}) copy-start(bf16[3,1536,256]{2,1,0:T(8,128)(2,1)} %param.19) | copy-start | bytes 7077892
  7.2 100.1 %all-gather.2.cloned.1.call-start = ((), (), s32[]{:S(2)}) async-start(), calls=%async_computation.3 | async-start | bytes 17825792 | tf_op jit(solution)/shard_map/all_gather | solution.py:84
  118.6 12.3 %copy-start.3 = (bf16[8,1,8192]{2,0,1:T(8,128)(2,1)S(1)}, bf16[8,1,8192]{2,0,1:T(8,128)(2,1)}, u32[]{:S(2)}) copy-start(bf16[8,1,8192]{2,0,1:T(8,128)(2,1)} %param.11) | copy-start | bytes 393220
  149.1 2.3 copy-start.1
  160.4 7.5 %copy-start.4 = (s32[8,16,8]{1,2,0:T(8,128)S(1)}, s32[8,16,8]{1,2,0:T(8,128)}, u32[]{:S(2)}) copy-start(s32[8,16,8]{1,2,0:T(8,128)} %param.20) | copy-start | bytes 12292
  162.7 53.9 %all-to-all-start = ((bf16[16,8,1,8192]{3,1,2,0:T(8,128)(2,1)}), bf16[16,8,1,8192]{3,1,2,0:T(8,128)(2,1)}, u32[]{:S(2)}, u32[]{:S(2)}) async-start(bf16[16,8,1,8192]{3,1,2,0:T(8,128)(2,1)} %stack.3), calls=%async_computation | async-start | bytes 4194304 | tf_op jit(solution)/shard_map/all_to_all | solution.py:20
  167.9 246.1 %all-reduce.2.cloned.1.call-start = ((), (), s32[]{:S(2)}) async-start(), calls=%async_computation.4 | async-start | bytes 18874368 | tf_op jit(solution)/shard_map/psum | solution.py:129
  168.8 47.9 %copy-start.2 = (bf16[8,16,256]{2,1,0:T(8,128)(2,1)S(1)}, bf16[8,16,256]{2,1,0:T(8,128)(2,1)}, u32[]{:S(2)}) copy-start(bf16[8,16,256]{2,1,0:T(8,128)(2,1)} %param.16) | copy-start | bytes 196612
  175.9 67.9 %copy-start.6 = (f32[256]{0:T(256)S(1)}, f32[256]{0:T(256)}, u32[]{:S(2)}) copy-start(f32[256]{0:T(256)} %param.17) | copy-start | bytes 3076
  426.4 15.8 %copy-start.5 = (f32[8,16,8]{1,2,0:T(8,128)S(1)}, f32[8,16,8]{1,2,0:T(8,128)}, u32[]{:S(2)}) copy-start(f32[8,16,8]{1,2,0:T(8,128)} %param.21) | copy-start | bytes 12292
  435.4 20.2 %all-to-all-start.2 = ((bf16[16,3,26,256]{3,2,1,0:T(8,128)(2,1)}), bf16[16,3,26,256]{3,2,1,0:T(8,128)(2,1)}, u32[]{:S(2)}, u32[]{:S(2)}) async-start(bf16[16,3,26,256]{3,2,1,0:T(8,128)(2,1)} %copy.99), calls=%async_computation.2 | async-start | bytes 1572864 | tf_op jit(solution)/shard_map/all_to_all | solution.py:134
Sparse Core Ops, SparseCore 0:
  10.3 96.8 all-gather.1
  280.0 133.9 all-reduce.1
